TPU v7x, 256 devices: a whole 4x4x8 slice. The times are simulated.
256 devices in a mesh: gx: 4 (over x), gy: 8 (over y, core), gz: 8 (over z).
Axes of the slice: x: 4, y: 4, z: 8, core: 2. Of those that a mesh axis runs over, the one named last changes fastest.
Arguments:
- fields: float32 [3, 64, 128, 1024], P(None, 'gx', 'gy', 'gz'), may hold values from -6 to 6
- diffusivity: float32 [64, 128, 1024], P('gx', 'gy', 'gz'), may hold values from 0.03 to 0.15
- velocity: float32 [3, 64, 128, 1024], P(None, 'gx', 'gy', 'gz'), may hold values from -2.4 to 2.4
- stored_snapshots: bfloat16 [127, 786432], P(None, ('gx', 'gy', 'gz')), may hold values from -36 to 36
- sample_index: int32 [262144], P(('gx', 'gy', 'gz')), may hold values from 0 to 32767, as said below
Outputs:
- new_fields: float32 [3, 64, 128, 1024], P(None, 'gx', 'gy', 'gz')
- snapshot_r: float32 [128, 128], replicated
Inputs may be any that keep to these rules, and one draw needn't show every extreme that they name: `sample_index`: entry k of a tile's list lies between k * 32 and (k + 1) * 32 - 1.
All inputs are finite; a program needn't handle non-finite values.
Results may differ from a plain program's by a relative error of at most 0.0003.
Values sent between devices are 32-bit elements; how exact they have to be, the bound alone decides.
A program may use at most 64 MiB of HBM per device.

v0:
```python
import jax
import jax.numpy as jnp
from jax import lax
from jax.sharding import PartitionSpec as P


def with_halo(array, sides, width):
    for axis, dim in sides:
        devices, length = (lax.axis_size(axis), array.shape[dim])
        up = [(i, (i + 1) % devices) for i in range(devices - 1)]
        down = [(j, i) for i, j in up]
        last = lax.slice_in_dim(array, length - width, length, axis=dim)
        first = lax.slice_in_dim(array, 0, width, axis=dim)
        before = lax.ppermute(last, axis, up)
        after = lax.ppermute(first, axis, down)
        array = jnp.concatenate([before, array, after], axis=dim)
    return array


def face_term(center_u, center_k, plus_u, plus_k, plus_v, minus_u, minus_k, minus_v):
    return (
        0.5 * (plus_k + center_k) * (plus_u - center_u)
        - 0.5 * (center_k + minus_k) * (center_u - minus_u)
        - 0.5 * (plus_v * plus_u - minus_v * minus_u)
    )


def upper_factor(gram):
    return jnp.linalg.cholesky(gram).T


def inner_rows(left, right):
    return lax.dot_general(
        left, right, (((1,), (1,)), ((), ())), preferred_element_type=jnp.float32
    )


def per_device(fields, diffusivity, velocity, stored_snapshots, sample_index):
    total_rows = (
        stored_snapshots.shape[1] * lax.axis_size("gx") * lax.axis_size("gy") * lax.axis_size("gz")
    )
    stacked = jnp.concatenate([fields, velocity, diffusivity[None]], 0)
    padded = with_halo(stacked, (("gx", 1), ("gy", 2), ("gz", 3)), 1)
    padded_u = padded[0:3]
    padded_v = padded[3:6]
    padded_k = padded[6]
    inner = (slice(1, -1), slice(1, -1), slice(1, -1))
    terms = []
    for dim in range(3):
        upper = list(inner)
        lower = list(inner)
        upper[dim] = slice(2, None)
        lower[dim] = slice(None, -2)
        upper = tuple(upper)
        lower = tuple(lower)
        terms.append(
            face_term(
                fields,
                diffusivity,
                padded_u[(slice(None),) + upper],
                padded_k[upper],
                padded_v[dim][upper],
                padded_u[(slice(None),) + lower],
                padded_k[lower],
                padded_v[dim][lower],
            )
        )
    new_fields = fields + (terms[0] + terms[1] + terms[2])
    flat_cells = new_fields.reshape(3, -1)
    sampled = jnp.take(flat_cells, sample_index, axis=1)
    new_column = sampled.reshape(1, -1).astype(jnp.bfloat16)
    snapshot_block = jnp.concatenate([stored_snapshots, new_column], 0)
    local_gram = inner_rows(snapshot_block, snapshot_block) / float(total_rows)
    whole_gram = lax.psum(local_gram, ("gx", "gy", "gz"))
    snapshot_r = upper_factor(whole_gram)
    return (new_fields, snapshot_r)


def solution(mesh):
    placed = (
        P(None, "gx", "gy", "gz"),
        P("gx", "gy", "gz"),
        P(None, "gx", "gy", "gz"),
        P(None, ("gx", "gy", "gz")),
        P(("gx", "gy", "gz")),
    )
    return jax.shard_map(
        per_device,
        mesh=mesh,
        in_specs=placed,
        out_specs=(P(None, "gx", "gy", "gz"), P()),
        check_vma=False,
    )
```

profile of v0, /device:TPU:1, one launch (start us, length us, event | category | flops | bytes accessed | tf_op | source)
XLA Modules:
  0.0 335.2 jit_solution(9069121309860138379)
XLA Ops:
  7.2 0.0 copy-start.3
  7.2 0.0 copy-start
  7.2 0.0 copy-start.1
  7.2 0.0 copy-start.11
  7.2 0.0 all-reduce.2.cloned.1.call-start
  7.3 0.9 pad_maximum_fusion.25
  8.2 3.9 %collective-permute-start = (f32[7,1,16,128]{3,2,1,0:T(8,128)S(1)}, f32[7,1,16,128]{3,2,1,0:T(8,128)S(1)}, u32[]{:S(2)}, u32[]{:S(2)}) collective-permute-start(f32[7,1,16,128]{3,2,1,0:T(8,128)S(1)} %get-tuple-element.18), channel_id=1, source_target_pairs={{0,64},{64,128},{128,192},{1,65},{65,129},{129,193},{2,66},{66,130... | collective-permute-start | bytes 172040 | tf_op jit(solution)/shard_map/ppermute | solution.py:14
  12.1 1.3 collective-permute-start.1
  13.4 0.0 collective-permute-done
  13.4 3.6 %collective-permute-done.1 = f32[7,1,16,128]{3,2,1,0:T(8,128)S(1)} collective-permute-done((f32[7,1,16,128]{3,2,1,0:T(8,128)S(1)}, f32[7,1,16,128]{3,2,1,0:T(8,128)S(1)}, u32[]{:S(2)}, u32[]{:S(2)}) %collective-permute-start.1) | collective-permute-done | bytes 57376 | tf_op jit(solution)/shard_map/ppermute | solution.py:15
  17.0 0.0 copy-start.5
  17.0 1.4 pad_maximum_fusion.22
  18.4 5.2 %collective-permute-start.2 = (f32[7,18,1,128]{3,2,1,0:T(1,128)S(1)}, f32[7,18,1,128]{3,2,1,0:T(1,128)S(1)}, u32[]{:S(2)}, u32[]{:S(2)}) collective-permute-start(f32[7,18,1,128]{3,2,1,0:T(1,128)S(1)} %get-tuple-element.16), channel_id=1, source_target_pairs={{0,8},{8,16},{16,24},{24,32},{32,40},{40,48},{48,56},{1,9},{9,17},... | collective-permute-start | bytes 193544 | tf_op jit(solution)/shard_map/ppermute | solution.py:14
  23.6 1.9 collective-permute-start.3
  25.6 0.0 copy-done.11
  25.6 0.0 collective-permute-done.2
  25.6 0.0 copy-start.7
  25.6 3.6 %collective-permute-done.3 = f32[7,18,1,128]{3,2,1,0:T(1,128)S(1)} collective-permute-done((f32[7,18,1,128]{3,2,1,0:T(1,128)S(1)}, f32[7,18,1,128]{3,2,1,0:T(1,128)S(1)}, u32[]{:S(2)}, u32[]{:S(2)}) %collective-permute-start.3) | collective-permute-done | bytes 64544 | tf_op jit(solution)/shard_map/ppermute | solution.py:15
  29.2 0.0 copy-done.5
  29.2 0.0 copy-done.7
  29.2 0.0 copy-start.9
  29.2 0.6 copy-done.9
  29.8 0.0 copy-done.3
  29.8 0.0 copy-done
  29.8 0.0 copy-done.1
  29.8 0.3 pad_maximum_fusion.1
  30.1 0.5 fusion.27
  30.6 1.6 copy.38
  32.2 3.5 %collective-permute-start.4 = (f32[7,18,18,1]{2,0,3,1:T(8,128)}, f32[7,18,18,1]{2,0,3,1:T(8,128)S(1)}, u32[]{:S(2)}, u32[]{:S(2)}) collective-permute-start(f32[7,18,18,1]{2,0,3,1:T(8,128)} %copy.38), channel_id=1, source_target_pairs={{0,1},{1,2},{2,3},{3,4},{4,5},{5,6},{6,7},{8,9},{9,10},{10,11},{11... | collective-permute-start | bytes 27224 | tf_op jit(solution)/shard_map/ppermute | solution.py:14
  35.7 1.0 copy.39
  36.7 1.5 collective-permute-start.5
  38.1 0.6 compare_and_fusion
  38.7 0.0 collective-permute-done.4
  38.7 0.9 copy.40
  39.6 2.4 collective-permute-done.5
  42.1 1.8 copy.41
  43.8 4.9 %pad_maximum_fusion = f32[7,18,18,130]{3,2,1,0:T(8,128)S(1)} fusion(f32[7,18,18,1]{3,2,1,0:T(8,128)S(1)} %copy.41, f32[7,18,1,128]{3,2,1,0:T(1,128)} %copy-done.9, f32[7,1,16,128]{3,2,1,0:T(8,128)} %copy-done.5, f32[1,16,16,128]{3,2,1,0:T(8,128)} %bitcast.24, f32[3,16,16,128]{3,2,1,0:T(8,128)} %param.7, f32[3,16,16,128]{3,2,1,0:T(8,128)S(1)} %copy-done, ...), kind=kLoop, calls=%fused_computation.1 | loop fusion | flops 2358720 | bytes 2358720 | tf_op jit(solution)/shard_map/concatenate | solution.py:16
  48.8 0.0 copy-start.4
  48.8 0.2 slice_bitcast_fusion.2
  48.9 0.7 copy-done.4
  49.7 0.0 copy-start.2
  49.7 0.0 copy-start.6
  49.7 0.3 fusion.23
  50.0 0.2 fusion.29
  50.2 0.5 copy-done.2
  50.7 0.0 copy-done.6
  50.7 0.0 copy-done.8
  50.7 0.0 copy-done.10
  50.7 1.5 add_add_fusion
  52.2 7.4 %copy.44 = bf16[3,16,16,128]{0,3,2,1:T(8,128)(2,1)} copy(f32[3,16,16,128]{3,2,1,0:T(8,128)} %add_add_fusion) | data formatting | bytes 589824 | tf_op jit(solution)/shard_map/add | solution.py:68
  59.6 7.3 %gather_fusion = bf16[1024,3]{1,0:T(8,128)(2,1)S(1)} fusion(bf16[3,32768]{0,1:T(8,128)(2,1)} %bitcast.21, s32[1024]{0:T(1024)S(1)} %fusion.25), kind=kCustom, calls=%fused_computation | custom fusion | bytes 16384 | tf_op jit(solution)/shard_map/jit(_take)/gather | solution.py:70
  66.9 0.0 copy-done.12
  66.9 0.2 fusion.17
  67.1 0.1 copy.45
  67.3 0.0 copy-done.13
  67.3 1.0 convolution_multiply_fusion
  68.3 0.0 all-reduce.2.cloned.1.call-update
  68.3 244.4 %all-reduce.2.cloned.1.call-done = f32[128,128]{0,1:T(8,128)} async-done(((f32[128,128]{0,1:T(8,128)}), f32[128,128]{0,1:T(8,128)}) %all-reduce.2.cloned.1.call-update) | async-done | bytes 65552 | tf_op jit(solution)/shard_map/psum | solution.py:74
  312.8 0.9 copy.47
  313.7 0.9 fusion.24
  314.6 11.7 %cholesky.18 = f32[128,128]{1,0:T(8,128)S(1)} custom-call(f32[128,128]{1,0:T(8,128)S(1)} %fusion.24), custom_call_target="Cholesky" | custom-call | tf_op jit(solution)/shard_map/jit(cholesky)/cholesky | solution.py:29
  326.3 0.6 compare_reduce_fusion
  327.0 0.7 select_bitcast_fusion
  327.6 0.7 copy.48
  (7 shorter events, 0.1 us)
Async XLA Ops:
  7.2 22.7 %copy-start.3 = (f32[16,16,128]{2,1,0:T(8,128)S(1)}, f32[16,16,128]{2,1,0:T(8,128)}, u32[]{:S(2)}) copy-start(f32[16,16,128]{2,1,0:T(8,128)} %param.6) | copy-start | bytes 393220
  7.2 22.7 %copy-start = (f32[3,16,16,128]{3,2,1,0:T(8,128)S(1)}, f32[3,16,16,128]{3,2,1,0:T(8,128)}, u32[]{:S(2)}) copy-start(f32[3,16,16,128]{3,2,1,0:T(8,128)} %param.5) | copy-start | bytes 1179652
  7.2 22.7 %copy-start.1 = (f32[3,16,16,128]{3,2,1,0:T(8,128)S(1)}, f32[3,16,16,128]{3,2,1,0:T(8,128)}, u32[]{:S(2)}) copy-start(f32[3,16,16,128]{3,2,1,0:T(8,128)} %param.7) | copy-start | bytes 1179652
  7.2 18.4 %copy-start.11 = (s32[1024]{0:T(1024)S(1)}, s32[1024]{0:T(1024)}, u32[]{:S(2)}) copy-start(s32[1024]{0:T(1024)} %param.9) | copy-start | bytes 12292
  7.2 305.6 %all-reduce.2.cloned.1.call-start = ((), (), s32[]{:S(2)}) async-start(), calls=%async_computation | async-start | bytes 131072 | tf_op jit(solution)/shard_map/psum | solution.py:74
  8.2 5.2 %collective-permute-start = (f32[7,1,16,128]{3,2,1,0:T(8,128)S(1)}, f32[7,1,16,128]{3,2,1,0:T(8,128)S(1)}, u32[]{:S(2)}, u32[]{:S(2)}) collective-permute-start(f32[7,1,16,128]{3,2,1,0:T(8,128)S(1)} %get-tuple-element.18), channel_id=1, source_target_pairs={{0,64},{64,128},{128,192},{1,65},{65,129},{129,193},{2,66},{66,130... | collective-permute-start | bytes 172040 | tf_op jit(solution)/shard_map/ppermute | solution.py:14
  12.1 4.9 %collective-permute-start.1 = (f32[7,1,16,128]{3,2,1,0:T(8,128)S(1)}, f32[7,1,16,128]{3,2,1,0:T(8,128)S(1)}, u32[]{:S(2)}, u32[]{:S(2)}) collective-permute-start(f32[7,1,16,128]{3,2,1,0:T(8,128)S(1)} %get-tuple-element.19), channel_id=1, source_target_pairs={{64,0},{128,64},{192,128},{65,1},{129,65},{193,129},{66,2},{130,66... | collective-permute-start | bytes 172040 | tf_op jit(solution)/shard_map/ppermute | solution.py:15
  17.0 12.2 %copy-start.5 = (f32[7,1,16,128]{3,2,1,0:T(8,128)}, f32[7,1,16,128]{3,2,1,0:T(8,128)S(1)}, u32[]{:S(2)}) copy-start(f32[7,1,16,128]{3,2,1,0:T(8,128)S(1)} %collective-permute-done.1) | copy-start | bytes 172036
  18.4 7.2 %collective-permute-start.2 = (f32[7,18,1,128]{3,2,1,0:T(1,128)S(1)}, f32[7,18,1,128]{3,2,1,0:T(1,128)S(1)}, u32[]{:S(2)}, u32[]{:S(2)}) collective-permute-start(f32[7,18,1,128]{3,2,1,0:T(1,128)S(1)} %get-tuple-element.16), channel_id=1, source_target_pairs={{0,8},{8,16},{16,24},{24,32},{32,40},{40,48},{48,56},{1,9},{9,17},... | collective-permute-start | bytes 193544 | tf_op jit(solution)/shard_map/ppermute | solution.py:14
  23.6 5.6 %collective-permute-start.3 = (f32[7,18,1,128]{3,2,1,0:T(1,128)S(1)}, f32[7,18,1,128]{3,2,1,0:T(1,128)S(1)}, u32[]{:S(2)}, u32[]{:S(2)}) collective-permute-start(f32[7,18,1,128]{3,2,1,0:T(1,128)S(1)} %get-tuple-element.17), channel_id=1, source_target_pairs={{8,0},{16,8},{24,16},{32,24},{40,32},{48,40},{56,48},{9,1},{17,9},... | collective-permute-start | bytes 193544 | tf_op jit(solution)/shard_map/ppermute | solution.py:15
  25.6 3.6 %copy-start.7 = (f32[7,18,1,128]{3,2,1,0:T(1,128)}, f32[7,18,1,128]{3,2,1,0:T(1,128)S(1)}, u32[]{:S(2)}) copy-start(f32[7,18,1,128]{3,2,1,0:T(1,128)S(1)} %collective-permute-done.2) | copy-start | bytes 193540
  29.2 0.6 copy-start.9
  32.2 6.5 %collective-permute-start.4 = (f32[7,18,18,1]{2,0,3,1:T(8,128)}, f32[7,18,18,1]{2,0,3,1:T(8,128)S(1)}, u32[]{:S(2)}, u32[]{:S(2)}) collective-permute-start(f32[7,18,18,1]{2,0,3,1:T(8,128)} %copy.38), channel_id=1, source_target_pairs={{0,1},{1,2},{2,3},{3,4},{4,5},{5,6},{6,7},{8,9},{9,10},{10,11},{11... | collective-permute-start | bytes 27224 | tf_op jit(solution)/shard_map/ppermute | solution.py:14
  36.7 5.4 %collective-permute-start.5 = (f32[7,18,18,1]{2,0,3,1:T(8,128)S(1)}, f32[7,18,18,1]{2,0,3,1:T(8,128)}, u32[]{:S(2)}, u32[]{:S(2)}) collective-permute-start(f32[7,18,18,1]{2,0,3,1:T(8,128)S(1)} %copy.39), channel_id=1, source_target_pairs={{1,0},{2,1},{3,2},{4,3},{5,4},{6,5},{7,6},{9,8},{10,9},{11,10},{12... | collective-permute-start | bytes 27224 | tf_op jit(solution)/shard_map/ppermute | solution.py:15
  48.8 0.9 copy-start.4
  49.7 1.0 copy-start.2
  49.7 1.0 copy-start.6
  49.7 1.0 copy-start.8
  49.7 1.0 copy-start.10
  52.2 14.8 %copy-start.12 = (pred[1024]{0:T(1024)(128)(4,1)S(1)}, pred[1024]{0:T(1024)(128)(4,1)}, u32[]{:S(2)}) copy-start(pred[1024]{0:T(1024)(128)(4,1)} %compare_and_fusion) | copy-start | bytes 3076
  52.2 15.1 %copy-start.13 = (bf16[127,3072]{1,0:T(8,128)(2,1)S(1)}, bf16[127,3072]{1,0:T(8,128)(2,1)}, u32[]{:S(2)}) copy-start(bf16[127,3072]{1,0:T(8,128)(2,1)} %param.8) | copy-start | bytes 2340868
Sparse Core Ops, SparseCore 0:
  68.5 244.2 all-reduce.1
where the time goes:
time: 336 us; the launch traced here: 335 us
  waiting for transfers between devices  254 us (76%)
  local copies, waits for them, and re-layouts  24.5 us (7%)
  other arithmetic  24 us (7%)
  starting transfers between devices  17.4 us (5%)
  between operations  14.3 us (4%)
    psum x1, waiting for transfers between devices, per_device(): whole_gram = lax.psum(local_gram, ('gx', 'gy', 'gz'))  244 us
    ppermute x3, starting transfers between devices, with_halo(): before = lax.ppermute(last, axis, up)  12.7 us
    another operation x3, other arithmetic, upper_factor(): return jnp.linalg.cholesky(gram).T  12.4 us
    ppermute x3, waiting for transfers between devices, with_halo(): after = lax.ppermute(first, axis, down)  9.65 us
    add x1, local copies, waits for them, and re-layouts, per_device(): new_fields = fields + (terms[0] + terms[1] + terms[2])  7.41 us
    gather x1, local copies, waits for them, and re-layouts, per_device(): sampled = jnp.take(flat_cells, sample_index, axis=1)  7.34 us
  transfers between devices with their start and end apart: 7, of which 4 were waited for; matrix products, arithmetic and copies ran while one was open for 1% of the time, Pallas kernels for 0%

commit v1 on v0

--- a/solution.py
+++ b/solution.py
@@ -71,7 +71,7 @@
     new_column = sampled.reshape(1, -1).astype(jnp.bfloat16)
     snapshot_block = jnp.concatenate([stored_snapshots, new_column], 0)
     local_gram = inner_rows(snapshot_block, snapshot_block) / float(total_rows)
-    whole_gram = lax.psum(local_gram, ("gx", "gy", "gz"))
+    whole_gram = jnp.sum(lax.all_gather(local_gram, ("gx", "gy", "gz")), axis=0)
     snapshot_r = upper_factor(whole_gram)
     return (new_fields, snapshot_r)
 

time: 336 us -> 225 us (0.67)
  waiting for transfers between devices: 254 us -> 138 us
  other arithmetic: 24 us -> 29.7 us
    psum x1 -> x0, waiting for transfers between devices: 244 us -> none  [per_device(): whole_gram = lax.psum(local_gram, ('gx', 'gy', 'gz'))]
    all_gather x0 -> x1, waiting for transfers between devices: none -> 128 us  [per_device(): whole_gram = jnp.sum(lax.all_gather(local_gram, ('gx', 'gy', 'gz')), axis=0)]
    reduce_sum x0 -> x1, other arithmetic: none -> 6.59 us  [per_device(): whole_gram = jnp.sum(lax.all_gather(local_gram, ('gx', 'gy', 'gz')), axis=0)]
where the time goes in v1:
time: 225 us
  waiting for transfers between devices  138 us (61%)
  other arithmetic  29.7 us (13%)
  local copies, waits for them, and re-layouts  23.6 us (10%)
  starting transfers between devices  18 us (8%)
  between operations  14.3 us (6%)
    all_gather x1, waiting for transfers between devices, per_device(): whole_gram = jnp.sum(lax.all_gather(local_gram, ('gx', 'gy', 'gz')), axis=0)  128 us
    ppermute x3, starting transfers between devices, with_halo(): before = lax.ppermute(last, axis, up)  13.3 us
    another operation x3, other arithmetic, upper_factor(): return jnp.linalg.cholesky(gram).T  12.4 us
    ppermute x3, waiting for transfers between devices, with_halo(): after = lax.ppermute(first, axis, down)  10.2 us
    add x1, local copies, waits for them, and re-layouts, per_device(): new_fields = fields + (terms[0] + terms[1] + terms[2])  7.39 us
    gather x1, local copies, waits for them, and re-layouts, per_device(): sampled = jnp.take(flat_cells, sample_index, axis=1)  7.34 us
    reduce_sum x1, other arithmetic, per_device(): whole_gram = jnp.sum(lax.all_gather(local_gram, ('gx', 'gy', 'gz')), axis=0)  6.59 us
    concatenate x2, other arithmetic, with_halo(): array = jnp.concatenate([before, array, after], axis=dim)  5.21 us
  transfers between devices with their start and end apart: 7, of which 4 were waited for; matrix products, arithmetic and copies ran while one was open for 1% of the time, Pallas kernels for 0%

profile of v1, /device:TPU:1, one launch (start us, length us, event | category | flops | bytes accessed | tf_op | source)
XLA Modules:
  0.0 224.6 jit_solution(6000943730295542074)
XLA Ops:
  7.2 0.0 copy-start.1
  7.2 0.0 copy-start
  7.2 0.0 copy-start.3
  7.2 0.0 copy-start.12
  7.2 0.0 all-gather.3.cloned.1.call-start
  7.3 0.9 pad_maximum_fusion.25
  8.1 3.9 %collective-permute-start = (f32[7,1,16,128]{3,2,1,0:T(8,128)S(1)}, f32[7,1,16,128]{3,2,1,0:T(8,128)S(1)}, u32[]{:S(2)}, u32[]{:S(2)}) collective-permute-start(f32[7,1,16,128]{3,2,1,0:T(8,128)S(1)} %get-tuple-element.18), channel_id=1, source_target_pairs={{0,64},{64,128},{128,192},{1,65},{65,129},{129,193},{2,66},{66,130... | collective-permute-start | bytes 172040 | tf_op jit(solution)/shard_map/ppermute | solution.py:14
  12.1 1.3 collective-permute-start.1
  13.4 0.0 collective-permute-done
  13.4 3.6 %collective-permute-done.1 = f32[7,1,16,128]{3,2,1,0:T(8,128)S(1)} collective-permute-done((f32[7,1,16,128]{3,2,1,0:T(8,128)S(1)}, f32[7,1,16,128]{3,2,1,0:T(8,128)S(1)}, u32[]{:S(2)}, u32[]{:S(2)}) %collective-permute-start.1) | collective-permute-done | bytes 57376 | tf_op jit(solution)/shard_map/ppermute | solution.py:15
  17.0 1.4 pad_maximum_fusion.22
  18.4 5.2 %collective-permute-start.2 = (f32[7,18,1,128]{3,2,1,0:T(1,128)S(1)}, f32[7,18,1,128]{3,2,1,0:T(1,128)S(1)}, u32[]{:S(2)}, u32[]{:S(2)}) collective-permute-start(f32[7,18,1,128]{3,2,1,0:T(1,128)S(1)} %get-tuple-element.16), channel_id=1, source_target_pairs={{0,8},{8,16},{16,24},{24,32},{32,40},{40,48},{48,56},{1,9},{9,17},... | collective-permute-start | bytes 193544 | tf_op jit(solution)/shard_map/ppermute | solution.py:14
  23.6 1.9 collective-permute-start.3
  25.5 0.0 copy-done.12
  25.6 0.0 collective-permute-done.2
  25.6 0.0 copy-start.7
  25.6 3.6 %collective-permute-done.3 = f32[7,18,1,128]{3,2,1,0:T(1,128)S(1)} collective-permute-done((f32[7,18,1,128]{3,2,1,0:T(1,128)S(1)}, f32[7,18,1,128]{3,2,1,0:T(1,128)S(1)}, u32[]{:S(2)}, u32[]{:S(2)}) %collective-permute-start.3) | collective-permute-done | bytes 64544 | tf_op jit(solution)/shard_map/ppermute | solution.py:15
  29.2 0.0 copy-done.5
  29.2 0.0 copy-done.7
  29.2 0.0 copy-start.9
  29.2 0.6 copy-done.9
  29.8 0.0 copy-done.1
  29.8 0.0 copy-done
  29.8 0.0 copy-done.3
  29.8 0.3 pad_maximum_fusion.1
  30.1 0.5 fusion.27
  30.6 1.6 copy.36
  32.2 0.0 copy-start.11
  32.2 0.9 copy.35
  33.1 4.2 %collective-permute-start.4 = (f32[7,18,18,1]{2,0,3,1:T(8,128)S(1)}, f32[7,18,18,1]{2,0,3,1:T(8,128)}, u32[]{:S(2)}, u32[]{:S(2)}) collective-permute-start(f32[7,18,18,1]{2,0,3,1:T(8,128)S(1)} %copy.35), channel_id=1, source_target_pairs={{0,1},{1,2},{2,3},{3,4},{4,5},{5,6},{6,7},{8,9},{9,10},{10,11},{11... | collective-permute-start | bytes 27224 | tf_op jit(solution)/shard_map/ppermute | solution.py:14
  37.3 0.0 copy-done.11
  37.3 1.5 collective-permute-start.5
  38.8 0.6 compare_and_fusion
  39.4 3.0 %collective-permute-done.5 = f32[7,18,18,1]{2,0,3,1:T(8,128)S(1)} collective-permute-done((f32[7,18,18,1]{2,0,3,1:T(8,128)S(1)}, f32[7,18,18,1]{2,0,3,1:T(8,128)S(1)}, u32[]{:S(2)}, u32[]{:S(2)}) %collective-permute-start.5) | collective-permute-done | bytes 9104 | tf_op jit(solution)/shard_map/ppermute | solution.py:15
  42.4 0.9 copy.38
  43.3 0.0 collective-permute-done.4
  43.3 1.8 copy.37
  45.0 4.9 %pad_maximum_fusion = f32[7,18,18,130]{3,2,1,0:T(8,128)S(1)} fusion(f32[7,18,18,1]{3,2,1,0:T(8,128)S(1)} %copy.38, f32[7,18,1,128]{3,2,1,0:T(1,128)} %copy-done.9, f32[7,1,16,128]{3,2,1,0:T(8,128)} %copy-done.5, f32[1,16,16,128]{3,2,1,0:T(8,128)} %bitcast.26, f32[3,16,16,128]{3,2,1,0:T(8,128)} %param.7, f32[3,16,16,128]{3,2,1,0:T(8,128)S(1)} %copy-done, ...), kind=kLoop, calls=%fused_computation.1 | loop fusion | flops 2358720 | bytes 2358720 | tf_op jit(solution)/shard_map/concatenate | solution.py:16
  50.0 0.0 copy-start.4
  50.0 0.2 slice_bitcast_fusion.2
  50.1 0.7 copy-done.4
  50.9 0.0 copy-start.2
  50.9 0.3 fusion.23
  51.2 0.2 fusion.29
  51.4 0.5 copy-done.2
  51.9 0.0 copy-done.6
  51.9 0.0 copy-done.8
  51.9 0.0 copy-done.10
  51.9 1.5 add_add_fusion
  53.4 7.4 %copy.41 = bf16[3,16,16,128]{0,3,2,1:T(8,128)(2,1)} copy(f32[3,16,16,128]{3,2,1,0:T(8,128)} %add_add_fusion) | data formatting | bytes 589824 | tf_op jit(solution)/shard_map/add | solution.py:68
  60.8 7.3 %gather_fusion = bf16[1024,3]{1,0:T(8,128)(2,1)S(1)} fusion(bf16[3,32768]{0,1:T(8,128)(2,1)} %bitcast.23, s32[1024]{0:T(1024)S(1)} %fusion.25), kind=kCustom, calls=%fused_computation | custom fusion | bytes 16384 | tf_op jit(solution)/shard_map/jit(_take)/gather | solution.py:70
  68.1 0.0 copy-done.13
  68.1 0.2 fusion.17
  68.3 0.1 copy.42
  68.5 0.0 copy-done.14
  68.5 1.0 convolution_multiply_fusion
  69.5 0.0 all-gather.3.cloned.1.call-update
  69.5 127.8 %all-gather.3.cloned.1.call-done = f32[32768,128]{1,0:T(8,128)} async-done(((f32[128,128]{1,0:T(8,128)}), f32[32768,128]{1,0:T(8,128)}) %all-gather.3.cloned.1.call-update) | async-done | bytes 16777232 | tf_op jit(solution)/shard_map/all_gather | solution.py:74
  197.3 6.6 %reduce_sum.9 = f32[128,128]{1,0:T(8,128)S(1)} reduce(f32[256,128,128]{2,1,0:T(8,128)} %bitcast.22, f32[]{:T(128)} %constant.56.clone.1), dimensions={0}, to_apply=%region_0.1 | reduce | flops 4177920 | bytes 16842756 | tf_op jit(solution)/shard_map/reduce_sum | solution.py:74
  203.9 0.1 copy.43
  204.0 11.7 %cholesky.18 = f32[128,128]{1,0:T(8,128)S(1)} custom-call(f32[128,128]{1,0:T(8,128)S(1)} %fusion.24), custom_call_target="Cholesky" | custom-call | tf_op jit(solution)/shard_map/jit(cholesky)/cholesky | solution.py:29
  215.8 0.6 compare_reduce_fusion
  216.4 0.7 select_bitcast_fusion
  217.1 0.7 copy.44
  (10 shorter events, 0.1 us)
Async XLA Ops:
  7.2 22.6 %copy-start.1 = (f32[3,16,16,128]{3,2,1,0:T(8,128)S(1)}, f32[3,16,16,128]{3,2,1,0:T(8,128)}, u32[]{:S(2)}) copy-start(f32[3,16,16,128]{3,2,1,0:T(8,128)} %param.7) | copy-start | bytes 1179652
  7.2 22.6 %copy-start = (f32[3,16,16,128]{3,2,1,0:T(8,128)S(1)}, f32[3,16,16,128]{3,2,1,0:T(8,128)}, u32[]{:S(2)}) copy-start(f32[3,16,16,128]{3,2,1,0:T(8,128)} %param.5) | copy-start | bytes 1179652
  7.2 22.6 %copy-start.3 = (f32[16,16,128]{2,1,0:T(8,128)S(1)}, f32[16,16,128]{2,1,0:T(8,128)}, u32[]{:S(2)}) copy-start(f32[16,16,128]{2,1,0:T(8,128)} %param.6) | copy-start | bytes 393220
  7.2 18.3 %copy-start.12 = (s32[1024]{0:T(1024)S(1)}, s32[1024]{0:T(1024)}, u32[]{:S(2)}) copy-start(s32[1024]{0:T(1024)} %param.9) | copy-start | bytes 12292
  7.2 190.1 %all-gather.3.cloned.1.call-start = ((), (), s32[]{:S(2)}) async-start(), calls=%async_computation | async-start | bytes 16842752 | tf_op jit(solution)/shard_map/all_gather | solution.py:74
  8.1 5.2 %collective-permute-start = (f32[7,1,16,128]{3,2,1,0:T(8,128)S(1)}, f32[7,1,16,128]{3,2,1,0:T(8,128)S(1)}, u32[]{:S(2)}, u32[]{:S(2)}) collective-permute-start(f32[7,1,16,128]{3,2,1,0:T(8,128)S(1)} %get-tuple-element.18), channel_id=1, source_target_pairs={{0,64},{64,128},{128,192},{1,65},{65,129},{129,193},{2,66},{66,130... | collective-permute-start | bytes 172040 | tf_op jit(solution)/shard_map/ppermute | solution.py:14
  12.1 4.9 %collective-permute-start.1 = (f32[7,1,16,128]{3,2,1,0:T(8,128)S(1)}, f32[7,1,16,128]{3,2,1,0:T(8,128)S(1)}, u32[]{:S(2)}, u32[]{:S(2)}) collective-permute-start(f32[7,1,16,128]{3,2,1,0:T(8,128)S(1)} %get-tuple-element.19), channel_id=1, source_target_pairs={{64,0},{128,64},{192,128},{65,1},{129,65},{193,129},{66,2},{130,66... | collective-permute-start | bytes 172040 | tf_op jit(solution)/shard_map/ppermute | solution.py:15
  17.0 12.2 %copy-start.5 = (f32[7,1,16,128]{3,2,1,0:T(8,128)}, f32[7,1,16,128]{3,2,1,0:T(8,128)S(1)}, u32[]{:S(2)}) copy-start(f32[7,1,16,128]{3,2,1,0:T(8,128)S(1)} %collective-permute-done.1) | copy-start | bytes 172036
  18.4 7.2 %collective-permute-start.2 = (f32[7,18,1,128]{3,2,1,0:T(1,128)S(1)}, f32[7,18,1,128]{3,2,1,0:T(1,128)S(1)}, u32[]{:S(2)}, u32[]{:S(2)}) collective-permute-start(f32[7,18,1,128]{3,2,1,0:T(1,128)S(1)} %get-tuple-element.16), channel_id=1, source_target_pairs={{0,8},{8,16},{16,24},{24,32},{32,40},{40,48},{48,56},{1,9},{9,17},... | collective-permute-start | bytes 193544 | tf_op jit(solution)/shard_map/ppermute | solution.py:14
  23.6 5.6 %collective-permute-start.3 = (f32[7,18,1,128]{3,2,1,0:T(1,128)S(1)}, f32[7,18,1,128]{3,2,1,0:T(1,128)S(1)}, u32[]{:S(2)}, u32[]{:S(2)}) collective-permute-start(f32[7,18,1,128]{3,2,1,0:T(1,128)S(1)} %get-tuple-element.17), channel_id=1, source_target_pairs={{8,0},{16,8},{24,16},{32,24},{40,32},{48,40},{56,48},{9,1},{17,9},... | collective-permute-start | bytes 193544 | tf_op jit(solution)/shard_map/ppermute | solution.py:15
  25.6 3.6 %copy-start.7 = (f32[7,18,1,128]{3,2,1,0:T(1,128)}, f32[7,18,1,128]{3,2,1,0:T(1,128)S(1)}, u32[]{:S(2)}) copy-start(f32[7,18,1,128]{3,2,1,0:T(1,128)S(1)} %collective-permute-done.2) | copy-start | bytes 193540
  29.2 0.6 copy-start.9
  32.2 5.1 %copy-start.11 = (f32[7,18,18,1]{2,0,3,1:T(8,128)S(1)}, f32[7,18,18,1]{2,0,3,1:T(8,128)}, u32[]{:S(2)}) copy-start(f32[7,18,18,1]{2,0,3,1:T(8,128)} %copy.36) | copy-start | bytes 27220
  33.1 10.2 %collective-permute-start.4 = (f32[7,18,18,1]{2,0,3,1:T(8,128)S(1)}, f32[7,18,18,1]{2,0,3,1:T(8,128)}, u32[]{:S(2)}, u32[]{:S(2)}) collective-permute-start(f32[7,18,18,1]{2,0,3,1:T(8,128)S(1)} %copy.35), channel_id=1, source_target_pairs={{0,1},{1,2},{2,3},{3,4},{4,5},{5,6},{6,7},{8,9},{9,10},{10,11},{11... | collective-permute-start | bytes 27224 | tf_op jit(solution)/shard_map/ppermute | solution.py:14
  37.3 5.1 %collective-permute-start.5 = (f32[7,18,18,1]{2,0,3,1:T(8,128)S(1)}, f32[7,18,18,1]{2,0,3,1:T(8,128)S(1)}, u32[]{:S(2)}, u32[]{:S(2)}) collective-permute-start(f32[7,18,18,1]{2,0,3,1:T(8,128)S(1)} %copy-done.11), channel_id=1, source_target_pairs={{1,0},{2,1},{3,2},{4,3},{5,4},{6,5},{7,6},{9,8},{10,9},{11,10},{12... | collective-permute-start | bytes 27224 | tf_op jit(solution)/shard_map/ppermute | solution.py:15
  50.0 0.9 copy-start.4
  50.9 1.0 copy-start.2
  50.9 1.0 copy-start.6
  50.9 1.0 copy-start.8
  50.9 1.0 copy-start.10
  53.4 14.7 %copy-start.13 = (pred[1024]{0:T(1024)(128)(4,1)S(1)}, pred[1024]{0:T(1024)(128)(4,1)}, u32[]{:S(2)}) copy-start(pred[1024]{0:T(1024)(128)(4,1)} %compare_and_fusion) | copy-start | bytes 3076
  53.4 15.1 %copy-start.14 = (bf16[127,3072]{1,0:T(8,128)(2,1)S(1)}, bf16[127,3072]{1,0:T(8,128)(2,1)}, u32[]{:S(2)}) copy-start(bf16[127,3072]{1,0:T(8,128)(2,1)} %param.8) | copy-start | bytes 2340868
Sparse Core Ops, SparseCore 0:
  69.7 127.6 all-gather.2
